TPU v7x, 1024 devices: a whole 4x4x32 slice. The times are simulated.
1024 devices in a mesh: pipe: 32 (over z), expert: 8 (over x_hi, y), dp: 4 (over x_lo, core).
Axes of the slice: x: 4 (x_hi: 2, x_lo: 2; x = x_hi * 2 + x_lo), y: 4, z: 32, core: 2. Of those that a mesh axis runs over, the one named last changes fastest.
Arguments:
- enter_fwd: bfloat16 [32, 1024, 7168], P('pipe', 'expert', 'dp'), may hold values from -6 to 6
- enter_rev: bfloat16 [32, 1024, 7168], P('pipe', 'expert', 'dp'), may hold values from -6 to 6
- cot_rev: bfloat16 [32, 1024, 7168], P('pipe', 'expert', 'dp'), may hold values from -0.1875 to 0.1875
- gain: bfloat16 [2, 32, 7168], P(None, 'pipe', 'dp'), may hold values from 0.5 to 1.5
- proj_down: bfloat16 [2, 32, 256, 7168], P(None, 'pipe', None, 'dp'), may hold values from -0.0625 to 0.0625
- proj_up: bfloat16 [2, 32, 256, 7168], P(None, 'pipe', None, 'dp'), may hold values from -0.375 to 0.375
- master: float32 [2, 32, 256, 7168], P(None, 'pipe', 'expert', 'dp'), may hold values from -0.125 to 0.125
- moment: bfloat16 [2, 32, 256, 7168], P(None, 'pipe', 'expert', 'dp'), may hold values from -6 to 6
- second: bfloat16 [2, 32, 256, 7168], P(None, 'pipe', 'expert', 'dp'), may hold values from 0.5 to 20
Outputs:
- leave_fwd: bfloat16 [32, 1024, 7168], P('pipe', 'expert', 'dp')
- codes: bfloat16 [2, 32, 256, 7168], P(None, 'pipe', 'expert', 'dp')
- scales: float32 [2, 32, 2, 56], P(None, 'pipe', None, 'dp')
All inputs are finite; a program needn't handle non-finite values.
Results may differ from a plain program's by a relative error of at most 0.0047.
The roundings to bfloat16 on the way count: a program that leaves them out, or rounds other values in their place, can miss the bound.
Values may be sent and summed in bfloat16 or wider, within the bound.
A program may use at most 32 MiB of HBM per device.

v0:
```python
import jax
import jax.numpy as jnp
from jax import lax
from jax.sharding import PartitionSpec as P

D = 7168


def shifted(block, axis, distance):
    devices = range(lax.axis_size(axis))
    route = [(i - distance, i) for i in devices if i - distance in devices]
    return lax.ppermute(block, axis, route)


def from_partner(block, axis, distance):
    count = lax.axis_size(axis)
    route = []
    for low in range(count):
        high = low | 1 << distance
        if high != low and high < count:
            route += [(low, high), (high, low)]
    return lax.ppermute(block, axis, route)


def prepare(rows, gain_row, down):
    scaled = (rows.astype(jnp.float32) * gain_row).astype(jnp.bfloat16)
    squares = jnp.sum(jnp.square(rows.astype(jnp.float32)), axis=-1)
    raw = jnp.einsum("td,rd->tr", scaled, down, preferred_element_type=jnp.float32)
    return (scaled, squares, raw)


def shards(enter_fwd, enter_rev, cot_rev, gain, proj_down, proj_up, master, moment, second):
    fwd_rows = enter_fwd[0]
    back_rows = enter_rev[0]
    back_cot = cot_rev[0]
    own_gain = gain[0, 0].astype(jnp.float32)
    own_down = proj_down[0, 0]
    own_upper = proj_up[0, 0]
    copy_gain = gain[1, 0].astype(jnp.float32)
    copy_down = proj_down[1, 0]
    copy_upper = proj_up[1, 0]
    width_local = fwd_rows.shape[1]
    latent = own_down.shape[0]
    fwd_scaled, fwd_squares, fwd_raw = prepare(fwd_rows, own_gain, own_down)
    back_scaled, back_squares, back_raw = prepare(back_rows, copy_gain, copy_down)
    back_dlat = jnp.einsum("td,rd->tr", back_cot, copy_upper, preferred_element_type=jnp.float32)
    fwd_raw, fwd_squares, back_raw, back_squares, back_dlat = lax.psum(
        (fwd_raw, fwd_squares, back_raw, back_squares, back_dlat), "dp"
    )
    rscale = lax.rsqrt(fwd_squares / D + 1e-06)
    hidden = (fwd_raw * rscale[:, None]).astype(jnp.bfloat16)
    result = (
        fwd_rows.astype(jnp.float32)
        + jnp.dot(hidden, own_upper, preferred_element_type=jnp.float32)
    ).astype(jnp.bfloat16)
    leaving = shifted(result, "pipe", 1)
    back_r = lax.rsqrt(back_squares / D + 1e-06)
    hidden_two = (back_raw * back_r[:, None]).astype(jnp.bfloat16)
    error = (back_dlat * back_r[:, None]).astype(jnp.bfloat16)
    experts = lax.axis_size("expert")
    rows_local = latent // experts
    grad_down = jnp.einsum("tr,td->rd", error, back_scaled, preferred_element_type=jnp.float32)
    grad_up = jnp.einsum("tr,td->rd", hidden_two, back_cot, preferred_element_type=jnp.float32)
    summed = lax.psum_scatter(
        jnp.concatenate([grad_down, grad_up], axis=1).astype(jnp.bfloat16),
        "expert",
        scatter_dimension=0,
        tiled=True,
    ).astype(jnp.float32)
    share = jnp.stack([summed[:, :width_local], summed[:, width_local:]]).astype(jnp.bfloat16)
    levels = lax.axis_size("pipe").bit_length() - 1
    bit_order = list(range(levels))
    for level in bit_order:
        share = from_partner(share, "pipe", level)
    grad = share.astype(jnp.float32)[:, None]
    first = 0.9 * moment.astype(jnp.float32) + 0.1 * grad
    secnd = 0.95 * second.astype(jnp.float32) + 0.05 * grad * grad
    update = first / (1.0 - 0.9**10) / (jnp.sqrt(secnd / (1.0 - 0.95**10)) + 1e-08)
    fresh = master - 0.01 * (update + 0.1 * master)
    col_blocks = width_local // 128
    local_peak = jnp.max(jnp.abs(fresh).reshape(2, rows_local, col_blocks, 128), axis=(1, 3))
    gathered = lax.all_gather(local_peak[None], "expert", axis=0, tiled=True)
    group = 128 // rows_local
    block_peak = jnp.max(gathered.reshape(experts // group, group, 2, col_blocks), axis=1) + 1e-06
    scale_rows = jnp.transpose(block_peak, (1, 0, 2))
    row_block = lax.axis_index("expert") * rows_local // 128
    mine = lax.dynamic_index_in_dim(block_peak, row_block, 0, keepdims=False)
    expanded = jnp.repeat(mine, 128, axis=-1)
    coded = (fresh / expanded[:, None, None, :]).astype(jnp.bfloat16)
    return (leaving[None], coded, scale_rows[:, None])


def solution(mesh):
    in_specs = (
        P("pipe", "expert", "dp"),
        P("pipe", "expert", "dp"),
        P("pipe", "expert", "dp"),
        P(None, "pipe", "dp"),
        P(None, "pipe", None, "dp"),
        P(None, "pipe", None, "dp"),
        P(None, "pipe", "expert", "dp"),
        P(None, "pipe", "expert", "dp"),
        P(None, "pipe", "expert", "dp"),
    )
    out_specs = (
        P("pipe", "expert", "dp"),
        P(None, "pipe", "expert", "dp"),
        P(None, "pipe", None, "dp"),
    )
    return jax.shard_map(shards, mesh=mesh, in_specs=in_specs, out_specs=out_specs, check_vma=False)
```

profile of v0, /device:TPU:6, one launch (start us, length us, event | category | flops | bytes accessed | tf_op | source)
XLA Modules:
  0.0 394.2 jit_solution(8986460988313531626)
XLA Ops:
  7.2 0.0 copy-start
  7.2 0.0 copy-start.2
  7.2 0.0 copy-start.3
  7.2 0.0 all-reduce.4.cloned.1.call-start
  7.2 0.9 convert_reduce_fusion
  8.2 2.4 fusion.9
  10.6 0.0 copy-done.2
  10.6 0.0 copy-start.1
  10.6 2.4 fusion.14
  13.0 0.0 copy-done
  13.0 0.0 copy-done.3
  13.0 1.1 fusion.11
  14.1 0.0 all-reduce.4.cloned.1.call-update
  14.1 0.0 reduce-scatter.2.cloned.1.call-start
  14.2 0.0 copy-done.1
  14.2 0.3 fusion.4
  14.4 6.2 %all-reduce = (f32[128]{0:T(128)S(1)}, f32[128]{0:T(128)S(1)}) all-reduce(f32[128]{0:T(128)S(1)} %get-tuple-element.25, f32[128]{0:T(128)S(1)} %get-tuple-element.26), channel_id=1, replica_groups=mesh['pipe'=32,'expert'=8,'dp'=4] {'dp'}, use_global_device_ids=true, to_apply=%region_2.0 | all-reduce | flops 256 | bytes 2048 | tf_op jit(solution)/shard_map/psum | solution.py:47
  20.6 73.7 %all-reduce.4.cloned.1.call-done = (f32[128,256]{1,0:T(8,128)}, f32[128,256]{1,0:T(8,128)}, f32[128,256]{1,0:T(8,128)}) async-done(((f32[128,256]{1,0:T(8,128)}, f32[128,256]{1,0:T(8,128)}, f32[128,256]{1,0:T(8,128)}), (f32[128,256]{1,0:T(8,128)}, f32[128,256]{1,0:T(8,128)}, f32[128,256]{1,0:T(8,128)})) %all-reduce.4.cloned.1.call-update) | async-done | bytes 393232 | tf_op jit(solution)/shard_map/psum | solution.py:47
  94.3 1.4 convolution_convert_fusion.1
  95.7 1.4 convolution_convert_fusion
  97.1 1.4 pad_maximum_fusion
  98.5 0.0 reduce-scatter.2.cloned.1.call-update
  98.5 0.0 copy-start.4
  98.5 0.0 copy-start.5
  98.5 113.3 %reduce-scatter.2.cloned.1.call-done = bf16[32,3584]{1,0:T(8,128)(2,1)} async-done(((bf16[256,3584]{1,0:T(8,128)(2,1)}), bf16[32,3584]{1,0:T(8,128)(2,1)}) %reduce-scatter.2.cloned.1.call-update) | async-done | bytes 229392 | tf_op jit(solution)/shard_map/reduce_scatter | solution.py:64
  211.8 1.0 slice_bitcast_fusion.1
  212.8 3.5 collective-permute-start.1
  216.3 4.4 %collective-permute-done.1 = bf16[2,32,1792]{2,1,0:T(8,128)(2,1)S(1)} collective-permute-done((bf16[2,32,1792]{2,1,0:T(8,128)(2,1)S(1)}, bf16[2,32,1792]{2,1,0:T(8,128)(2,1)S(1)}, u32[]{:S(2)}, u32[]{:S(2)}) %collective-permute-start.1) | collective-permute-done | bytes 229408 | tf_op jit(solution)/shard_map/ppermute | solution.py:22
  220.7 4.4 %collective-permute-start.2 = (bf16[2,32,1792]{2,1,0:T(8,128)(2,1)S(1)}, bf16[2,32,1792]{2,1,0:T(8,128)(2,1)S(1)}, u32[]{:S(2)}, u32[]{:S(2)}) collective-permute-start(bf16[2,32,1792]{2,1,0:T(8,128)(2,1)S(1)} %collective-permute-done.1), channel_id=1, source_target_pairs={{0,64},{64,0},{32,96},{96,32},{128,192},{192,128},{160,224},{224,1... | collective-permute-start | bytes 688136 | tf_op jit(solution)/shard_map/ppermute | solution.py:22
  225.2 7.4 %collective-permute-done.2 = bf16[2,32,1792]{2,1,0:T(8,128)(2,1)S(1)} collective-permute-done((bf16[2,32,1792]{2,1,0:T(8,128)(2,1)S(1)}, bf16[2,32,1792]{2,1,0:T(8,128)(2,1)S(1)}, u32[]{:S(2)}, u32[]{:S(2)}) %collective-permute-start.2) | collective-permute-done | bytes 229408 | tf_op jit(solution)/shard_map/ppermute | solution.py:22
  232.6 9.5 %collective-permute-start.3 = (bf16[2,32,1792]{2,1,0:T(8,128)(2,1)S(1)}, bf16[2,32,1792]{2,1,0:T(8,128)(2,1)S(1)}, u32[]{:S(2)}, u32[]{:S(2)}) collective-permute-start(bf16[2,32,1792]{2,1,0:T(8,128)(2,1)S(1)} %collective-permute-done.2), channel_id=1, source_target_pairs={{0,128},{128,0},{32,160},{160,32},{64,192},{192,64},{96,224},{224,... | collective-permute-start | bytes 688136 | tf_op jit(solution)/shard_map/ppermute | solution.py:22
  242.1 2.0 fusion
  244.1 1.3 collective-permute-start
  245.4 11.9 %collective-permute-done.3 = bf16[2,32,1792]{2,1,0:T(8,128)(2,1)S(1)} collective-permute-done((bf16[2,32,1792]{2,1,0:T(8,128)(2,1)S(1)}, bf16[2,32,1792]{2,1,0:T(8,128)(2,1)S(1)}, u32[]{:S(2)}, u32[]{:S(2)}) %collective-permute-start.3) | collective-permute-done | bytes 229408 | tf_op jit(solution)/shard_map/ppermute | solution.py:22
  257.3 20.5 %collective-permute-start.4 = (bf16[2,32,1792]{2,1,0:T(8,128)(2,1)S(1)}, bf16[2,32,1792]{2,1,0:T(8,128)(2,1)S(1)}, u32[]{:S(2)}, u32[]{:S(2)}) collective-permute-start(bf16[2,32,1792]{2,1,0:T(8,128)(2,1)S(1)} %collective-permute-done.3), channel_id=1, source_target_pairs={{0,256},{256,0},{32,288},{288,32},{64,320},{320,64},{96,352},{352,... | collective-permute-start | bytes 688136 | tf_op jit(solution)/shard_map/ppermute | solution.py:22
  277.8 30.7 %collective-permute-done.4 = bf16[2,32,1792]{2,1,0:T(8,128)(2,1)S(1)} collective-permute-done((bf16[2,32,1792]{2,1,0:T(8,128)(2,1)S(1)}, bf16[2,32,1792]{2,1,0:T(8,128)(2,1)S(1)}, u32[]{:S(2)}, u32[]{:S(2)}) %collective-permute-start.4) | collective-permute-done | bytes 229408 | tf_op jit(solution)/shard_map/ppermute | solution.py:22
  308.5 11.8 %collective-permute-start.5 = (bf16[2,32,1792]{2,1,0:T(8,128)(2,1)S(1)}, bf16[2,32,1792]{2,1,0:T(8,128)(2,1)S(1)}, u32[]{:S(2)}, u32[]{:S(2)}) collective-permute-start(bf16[2,32,1792]{2,1,0:T(8,128)(2,1)S(1)} %collective-permute-done.4), channel_id=1, source_target_pairs={{0,512},{512,0},{32,544},{544,32},{64,576},{576,64},{96,608},{608,... | collective-permute-start | bytes 688136 | tf_op jit(solution)/shard_map/ppermute | solution.py:22
  320.3 0.0 collective-permute-done
  320.3 35.8 %collective-permute-done.5 = bf16[2,32,1792]{2,1,0:T(8,128)(2,1)S(1)} collective-permute-done((bf16[2,32,1792]{2,1,0:T(8,128)(2,1)S(1)}, bf16[2,32,1792]{2,1,0:T(8,128)(2,1)S(1)}, u32[]{:S(2)}, u32[]{:S(2)}) %collective-permute-start.5) | collective-permute-done | bytes 229408 | tf_op jit(solution)/shard_map/ppermute | solution.py:22
  356.1 0.0 copy-done.4
  356.1 0.0 copy-done.5
  356.1 1.4 abs_reduce_fusion
  357.5 0.1 reduce_max.27
  357.6 27.6 %all-gather.1 = f32[8,2,14]{2,1,0:T(2,128)S(1)} all-gather(f32[1,2,14]{2,1,0:T(2,128)S(1)} %bitcast.106), channel_id=2, replica_groups=mesh['pipe'=32,'expert'=8,'dp'=4] {'expert'}, dimensions={0}, use_global_device_ids=true | all-gather | bytes 1008 | tf_op jit(solution)/shard_map/all_gather | solution.py:82
  385.2 0.1 broadcast_bitcast_fusion
  385.3 0.6 copy.30
  385.9 0.7 fusion.42
  386.6 0.8 copy.40
  (8 shorter events, 0.1 us)
Async XLA Ops:
  7.2 5.8 %copy-start = (bf16[1,128,1792]{2,1,0:T(8,128)(2,1)S(1)}, bf16[1,128,1792]{2,1,0:T(8,128)(2,1)}, u32[]{:S(2)}) copy-start(bf16[1,128,1792]{2,1,0:T(8,128)(2,1)} %param.11) | copy-start | bytes 1376260
  7.2 3.4 copy-start.2
  7.2 5.8 %copy-start.3 = (bf16[2,1,256,1792]{3,2,1,0:T(8,128)(2,1)S(1)}, bf16[2,1,256,1792]{3,2,1,0:T(8,128)(2,1)}, u32[]{:S(2)}) copy-start(bf16[2,1,256,1792]{3,2,1,0:T(8,128)(2,1)} %param.14) | copy-start | bytes 5505028
  7.2 87.1 %all-reduce.4.cloned.1.call-start = ((), (), s32[]{:S(2)}) async-start(), calls=%async_computation.2 | async-start | bytes 786432 | tf_op jit(solution)/shard_map/psum | solution.py:47
  10.6 3.6 copy-start.1
  14.1 197.7 %reduce-scatter.2.cloned.1.call-start = ((), (), s32[]{:S(2)}) async-start(), calls=%async_computation.1 | async-start | bytes 2064384 | tf_op jit(solution)/shard_map/reduce_scatter | solution.py:64
  98.5 257.6 %copy-start.4 = (f32[2,1,32,1792]{3,2,1,0:T(8,128)S(1)}, f32[2,1,32,1792]{3,2,1,0:T(8,128)}, u32[]{:S(2)}) copy-start(f32[2,1,32,1792]{3,2,1,0:T(8,128)} %param.15) | copy-start | bytes 1376260
  98.5 257.6 %copy-start.5 = (bf16[2,1,32,1792]{3,2,1,0:T(8,128)(2,1)S(1)}, bf16[2,1,32,1792]{3,2,1,0:T(8,128)(2,1)}, u32[]{:S(2)}) copy-start(bf16[2,1,32,1792]{3,2,1,0:T(8,128)(2,1)} %param.17) | copy-start | bytes 688132
  212.8 7.9 %collective-permute-start.1 = (bf16[2,32,1792]{2,1,0:T(8,128)(2,1)S(1)}, bf16[2,32,1792]{2,1,0:T(8,128)(2,1)S(1)}, u32[]{:S(2)}, u32[]{:S(2)}) collective-permute-start(bf16[2,32,1792]{2,1,0:T(8,128)(2,1)S(1)} %pad_maximum_fusion.1), channel_id=1, source_target_pairs={{0,32},{32,0},{64,96},{96,64},{128,160},{160,128},{192,224},{224,1... | collective-permute-start | bytes 688136 | tf_op jit(solution)/shard_map/ppermute | solution.py:22
  220.7 11.9 %collective-permute-start.2 = (bf16[2,32,1792]{2,1,0:T(8,128)(2,1)S(1)}, bf16[2,32,1792]{2,1,0:T(8,128)(2,1)S(1)}, u32[]{:S(2)}, u32[]{:S(2)}) collective-permute-start(bf16[2,32,1792]{2,1,0:T(8,128)(2,1)S(1)} %collective-permute-done.1), channel_id=1, source_target_pairs={{0,64},{64,0},{32,96},{96,32},{128,192},{192,128},{160,224},{224,1... | collective-permute-start | bytes 688136 | tf_op jit(solution)/shard_map/ppermute | solution.py:22
  232.6 24.7 %collective-permute-start.3 = (bf16[2,32,1792]{2,1,0:T(8,128)(2,1)S(1)}, bf16[2,32,1792]{2,1,0:T(8,128)(2,1)S(1)}, u32[]{:S(2)}, u32[]{:S(2)}) collective-permute-start(bf16[2,32,1792]{2,1,0:T(8,128)(2,1)S(1)} %collective-permute-done.2), channel_id=1, source_target_pairs={{0,128},{128,0},{32,160},{160,32},{64,192},{192,64},{96,224},{224,... | collective-permute-start | bytes 688136 | tf_op jit(solution)/shard_map/ppermute | solution.py:22
  244.1 76.2 %collective-permute-start = (bf16[128,1792]{1,0:T(8,128)(2,1)}, bf16[128,1792]{1,0:T(8,128)(2,1)S(1)}, u32[]{:S(2)}, u32[]{:S(2)}) collective-permute-start(bf16[128,1792]{1,0:T(8,128)(2,1)} %fusion), channel_id=1, source_target_pairs={{0,32},{32,64},{64,96},{96,128},{128,160},{160,192},{192,224},{224... | collective-permute-start | bytes 1376264 | tf_op jit(solution)/shard_map/ppermute | solution.py:12
  257.3 51.2 %collective-permute-start.4 = (bf16[2,32,1792]{2,1,0:T(8,128)(2,1)S(1)}, bf16[2,32,1792]{2,1,0:T(8,128)(2,1)S(1)}, u32[]{:S(2)}, u32[]{:S(2)}) collective-permute-start(bf16[2,32,1792]{2,1,0:T(8,128)(2,1)S(1)} %collective-permute-done.3), channel_id=1, source_target_pairs={{0,256},{256,0},{32,288},{288,32},{64,320},{320,64},{96,352},{352,... | collective-permute-start | bytes 688136 | tf_op jit(solution)/shard_map/ppermute | solution.py:22
  308.5 47.6 %collective-permute-start.5 = (bf16[2,32,1792]{2,1,0:T(8,128)(2,1)S(1)}, bf16[2,32,1792]{2,1,0:T(8,128)(2,1)S(1)}, u32[]{:S(2)}, u32[]{:S(2)}) collective-permute-start(bf16[2,32,1792]{2,1,0:T(8,128)(2,1)S(1)} %collective-permute-done.4), channel_id=1, source_target_pairs={{0,512},{512,0},{32,544},{544,32},{64,576},{576,64},{96,608},{608,... | collective-permute-start | bytes 688136 | tf_op jit(solution)/shard_map/ppermute | solution.py:22
Sparse Core Ops, SparseCore 0:
  14.2 80.0 all-reduce.3
  100.1 111.6 reduce-scatter.1
where the time goes:
time: 395 us; the launch traced here: 394 us
  waiting for transfers between devices  277 us (70%)
  starting transfers between devices  51.1 us (13%)
  blocking collectives  33.8 us (9%)
  between operations  14.2 us (4%)
  matrix products  10.7 us (3%)
  other arithmetic  4.79 us (1%)
    reduce_scatter x1, waiting for transfers between devices, shards(): lax.psum_scatter(jnp.concatenate([grad_down, grad_up], axis=1).astype(jnp...  113 us
    ppermute x5, waiting for transfers between devices, from_partner(): return lax.ppermute(block, axis, route)  90.2 us
    psum x1, waiting for transfers between devices, shards(): lax.psum((fwd_raw, fwd_squares, back_raw, back_squares, back_dlat), 'dp')  73.7 us
    ppermute x5, starting transfers between devices, from_partner(): return lax.ppermute(block, axis, route)  49.7 us
    all_gather x1, blocking collectives, shards(): gathered = lax.all_gather(local_peak[None], 'expert', axis=0, tiled=True)  27.6 us
  transfers between devices with their start and end apart: 8, of which 7 were waited for; matrix products, arithmetic and copies ran while one was open for 1% of the time, Pallas kernels for 0%

commit v1 on v0

v1 whole, which is shorter than its diff:
```python
import functools

import jax
import jax.numpy as jnp
from jax import lax
from jax.experimental import pallas as pl
from jax.experimental.pallas import tpu as pltpu
from jax.sharding import PartitionSpec as P

D = 7168
CW = 256
F32 = jnp.float32
BF16 = jnp.bfloat16
MESH = pl.DeviceIdType.MESH
NT = (((1,), (1,)), ((), ()))


def kernel(
    sections, chunks,
    x1_hbm, x2_hbm, c2_hbm, gain_hbm, down_hbm, up_hbm, master_hbm, moment_hbm, second_hbm,
    leave_hbm, codes_hbm, scales_ref,
    x1, x2, c2, gain, down, up, master, moment, second,
    xg2, part, core_got, chip_sum, near_got, lat, sq, sq_got, rows_r,
    ybuf, turned, grads, group_got, share, mirror_got, fresh, peak, peak_got, coded,
    load_sem, core_send, core_recv, near_send, near_recv, lat_send, lat_recv, sq_send, sq_recv,
    y_send, y_recv, zero_sem, group_send, group_recv, mirror_send, mirror_recv,
    peak_send, peak_recv, code_sem,
):
    pipe = lax.axis_index("pipe")
    expert = lax.axis_index("expert")
    dp = lax.axis_index("dp")
    core = lax.rem(dp, 2)
    other_core = {"dp": dp + 1 - 2 * core}
    near = {"dp": lax.rem(dp + 2, 4)}
    near_other = {"dp": 3 - dp}
    x_hi = expert // 4
    y = lax.rem(expert, 4)
    mirror = {"pipe": sections - 1 - pipe}
    following = {"pipe": lax.rem(pipe + 1, sections)}
    previous = {"pipe": lax.rem(pipe + sections - 1, sections)}
    peers = []
    for dx in range(2):
        for dy in range(4):
            if dx or dy:
                peers.append(lax.rem(x_hi + dx, 2) * 4 + lax.rem(y + dy, 4))

    loads = [
        (x1_hbm, x1), (gain_hbm, gain), (down_hbm.at[0], down.at[0]),
        (x2_hbm, x2), (down_hbm.at[1], down.at[1]), (c2_hbm, c2), (up_hbm.at[1], up.at[1]),
        (up_hbm.at[0], up.at[0]), (master_hbm, master), (moment_hbm, moment), (second_hbm, second),
    ]
    copies = [pltpu.make_async_copy(s, d, load_sem.at[i]) for i, (s, d) in enumerate(loads)]
    for copy in copies:
        copy.start()

    barrier = pltpu.get_barrier_semaphore()
    others = [other_core, near, near_other, mirror, following, previous]
    others += [{"expert": peer} for peer in peers]
    for device in others:
        pl.semaphore_signal(barrier, inc=1, device_id=device, device_id_type=MESH)

    def send(src, dst, send_sem, recv_sem, device):
        copy = pltpu.make_async_remote_copy(
            src_ref=src, dst_ref=dst, send_sem=send_sem, recv_sem=recv_sem,
            device_id=device, device_id_type=MESH,
        )
        copy.start()
        return copy

    def spread(column):
        return jnp.broadcast_to(column, (128, 128)).T[0:8]

    def project(rows_ref, gain_row, weights):
        rows = rows_ref[...].astype(F32)
        scaled = (rows * gain_row).astype(BF16)
        raw = lax.dot_general(scaled, weights, NT, preferred_element_type=F32)
        return scaled, raw, jnp.sum(rows * rows, axis=1, keepdims=True)

    for i in range(3):
        copies[i].wait()
    _, raw, square = project(x1, gain[0:1, :].astype(F32), down[0])
    part[0] = raw.reshape(2, 64, 256)
    sq[0] = spread(square)
    for i in range(3, 5):
        copies[i].wait()
    scaled, raw, square = project(x2, gain[1:2, :].astype(F32), down[1])
    xg2[...] = scaled
    part[1] = raw.reshape(2, 64, 256)
    sq[1] = spread(square)
    for i in range(5, 7):
        copies[i].wait()
    raw = lax.dot_general(c2[...], up[1], NT, preferred_element_type=F32)
    part[2] = raw.reshape(2, 64, 256)

    pl.semaphore_wait(barrier, len(others))

    pending = []
    for i in range(3):
        pending.append(send(part.at[i, 1 - core], core_got.at[i], core_send.at[i], core_recv.at[i], other_core))
    for i, device in enumerate((other_core, near, near_other)):
        pending.append(send(sq, sq_got.at[i], sq_send.at[i], sq_recv.at[i], device))
    near_copies = []
    for i in range(3):
        pending[i].wait_recv()
        chip_sum[i] = part[i, core] + core_got[i]
        near_copies.append(send(chip_sum.at[i], near_got.at[i], near_send.at[i], near_recv.at[i], near))
    for i in range(3, 6):
        pending[i].wait_recv()
    for s in range(2):
        total = (sq[s] + sq_got[0, s]) + (sq_got[1, s] + sq_got[2, s])
        scale = lax.rsqrt(total / D + 1e-06)
        turned_rows = jnp.broadcast_to(scale[0:1], (128, 128)).T
        rows_r[s] = turned_rows.reshape(2, 64, 128)
    lat_copies = []
    for i in range(3):
        near_copies[i].wait_recv()
        r = rows_r[min(i, 1), core]
        total = chip_sum[i] + near_got[i]
        lat[i, core] = (total * jnp.concatenate([r, r], axis=1)).astype(BF16)
        lat_copies.append(send(lat.at[i, core], lat.at[i, core], lat_send.at[i], lat_recv.at[i], other_core))

    copies[7].wait()
    lat_copies[0].wait_recv()
    hidden = lat[0].reshape(128, 256)

    def columns(k):
        return pl.ds(pl.multiple_of(k * CW, CW), CW)

    def y_copy(k):
        return pltpu.make_async_remote_copy(
            src_ref=ybuf.at[k], dst_ref=leave_hbm.at[:, columns(k)],
            send_sem=y_send.at[k], recv_sem=y_recv.at[k],
            device_id=following, device_id_type=MESH,
        )

    @pl.loop(0, chunks)
    def _(k):
        wide = jnp.dot(hidden, up[0, :, columns(k)], preferred_element_type=F32)
        ybuf[k] = (x1[:, columns(k)].astype(F32) + wide).astype(BF16)

        @pl.when(pipe < sections - 1)
        def _():
            y_copy(k).start()

    for i in (1, 2):
        lat_copies[i].wait_recv()
        turned[i - 1] = lat[i].reshape(128, 256).astype(F32).T.astype(BF16)

    @pl.loop(0, chunks)
    def _(k):
        grad_down = jnp.dot(turned[1], xg2[:, columns(k)], preferred_element_type=F32)
        grads[k, :, 0:32, :] = grad_down.astype(BF16).reshape(8, 32, CW)
        grad_up = jnp.dot(turned[0], c2[:, columns(k)], preferred_element_type=F32)
        grads[k, :, 32:64, :] = grad_up.astype(BF16).reshape(8, 32, CW)
        for slot, peer in enumerate(peers):
            send(grads.at[k, peer], group_got.at[k, slot], group_send.at[k], group_recv.at[k], {"expert": peer})

    def mirror_copy(k):
        return pltpu.make_async_remote_copy(
            src_ref=share.at[k], dst_ref=mirror_got.at[k],
            send_sem=mirror_send.at[k], recv_sem=mirror_recv.at[k],
            device_id=mirror, device_id_type=MESH,
        )

    @pl.loop(0, chunks)
    def _(k):
        pltpu.make_async_copy(group_got.at[k], group_got.at[k], group_recv.at[k]).wait()
        total = grads[k, expert].astype(F32)
        for slot in range(7):
            total = total + group_got[k, slot].astype(F32)
        share[k] = total.astype(BF16)
        mirror_copy(k).start()

    for i in range(8, 11):
        copies[i].wait()

    def update(k):
        mirror_copy(k).wait_recv()
        grad = mirror_got[k].astype(F32)
        first = 0.9 * moment[:, columns(k)].astype(F32) + 0.1 * grad
        secnd = 0.95 * second[:, columns(k)].astype(F32) + 0.05 * grad * grad
        step = first / (1.0 - 0.9**10) / (jnp.sqrt(secnd / (1.0 - 0.95**10)) + 1e-08)
        old = master[:, columns(k)]
        new = old - 0.01 * (step + 0.1 * old)
        fresh[k] = new
        size = jnp.abs(new)
        top = jnp.broadcast_to(jnp.max(size[0:32], axis=0, keepdims=True), (8, CW))
        low = jnp.broadcast_to(jnp.max(size[32:64], axis=0, keepdims=True), (8, CW))
        row = lax.broadcasted_iota(jnp.int32, (8, CW), 0)
        peak[k] = jnp.where(row < 4, top, low)
        for slot, peer in enumerate(peers):
            send(peak.at[k], peak_got.at[k, slot], peak_send.at[k], peak_recv.at[k], {"expert": peer})

    lane = lax.broadcasted_iota(jnp.int32, (8, 128), 1)

    def code_copy(k):
        return pltpu.make_async_copy(coded.at[k], codes_hbm.at[:, columns(k)], code_sem.at[k])

    def finish(k, tables):
        pltpu.make_async_copy(peak_got.at[k], peak_got.at[k], peak_recv.at[k]).wait()
        mine = peak[k]
        for slot in range(3):
            mine = jnp.maximum(mine, peak_got[k, slot])
        theirs = peak_got[k, 3]
        for slot in range(4, 7):
            theirs = jnp.maximum(theirs, peak_got[k, slot])
        mine_table, their_table = tables
        for block in range(CW // 128):
            cols = slice(block * 128, block * 128 + 128)
            own = jnp.max(mine[:, cols], axis=1, keepdims=True) + 1e-06
            far = jnp.max(theirs[:, cols], axis=1, keepdims=True) + 1e-06
            here = lane == k * (CW // 128) + block
            mine_table = jnp.where(here, own, mine_table)
            their_table = jnp.where(here, far, their_table)
            coded[k, 0:32, cols] = (fresh[k, 0:32, cols] / own[0:1]).astype(BF16)
            coded[k, 32:64, cols] = (fresh[k, 32:64, cols] / own[4:5]).astype(BF16)
        code_copy(k).start()
        return mine_table, their_table

    update(0)
    empty = jnp.zeros((8, 128), F32)

    def both(k, tables):
        update(k)
        return finish(k - 1, tables)

    tables = lax.fori_loop(1, chunks, both, (empty, empty))
    mine_table, their_table = finish(chunks - 1, tables)
    width = scales_ref.shape[-1]
    for m in range(2):
        for rb in range(2):
            row = jnp.where(x_hi == rb, mine_table[4 * m : 4 * m + 1], their_table[4 * m : 4 * m + 1])
            scales_ref[m, rb : rb + 1, :] = row[:, 0:width]

    for copy in pending + near_copies + lat_copies:
        copy.wait_send()

    @pl.when(pipe == 0)
    def _():
        ybuf_zero = jnp.zeros((128, CW), BF16)

        @pl.loop(0, chunks)
        def _(k):
            y_copy(k).wait_send()
            ybuf[k] = ybuf_zero
            copy = pltpu.make_async_copy(ybuf.at[k], leave_hbm.at[:, columns(k)], zero_sem)
            copy.start()
            copy.wait()

    @pl.when(pipe > 0)
    def _():
        @pl.loop(0, chunks)
        def _(k):
            y_copy(k).wait_recv()

            @pl.when(pipe < sections - 1)
            def _():
                y_copy(k).wait_send()

    @pl.loop(0, chunks)
    def _(k):
        pltpu.make_async_copy(group_got.at[k], group_got.at[k], group_send.at[k]).wait()
        pltpu.make_async_copy(peak_got.at[k], peak_got.at[k], peak_send.at[k]).wait()
        mirror_copy(k).wait_send()
        code_copy(k).wait()


def solution(mesh):
    sections = mesh.shape["pipe"]

    def shards(enter_fwd, enter_rev, cot_rev, gain, proj_down, proj_up, master, moment, second):
        width = enter_fwd.shape[-1]
        tokens = enter_fwd.shape[1]
        latent = proj_down.shape[2]
        rows = master.shape[2]
        chunks = width // CW
        any_spec = pl.BlockSpec(memory_space=pl.ANY)
        dma = pltpu.SemaphoreType.DMA
        leave, codes, scales = pl.pallas_call(
            functools.partial(kernel, sections, chunks),
            out_shape=(
                jax.ShapeDtypeStruct((tokens, width), BF16),
                jax.ShapeDtypeStruct((2 * rows, width), BF16),
                jax.ShapeDtypeStruct((2, 2, width // 128), F32),
            ),
            in_specs=[any_spec] * 9,
            out_specs=(any_spec, any_spec, pl.BlockSpec(memory_space=pltpu.VMEM)),
            scratch_shapes=[
                pltpu.VMEM((tokens, width), BF16),
                pltpu.VMEM((tokens, width), BF16),
                pltpu.VMEM((tokens, width), BF16),
                pltpu.VMEM((2, width), BF16),
                pltpu.VMEM((2, latent, width), BF16),
                pltpu.VMEM((2, latent, width), BF16),
                pltpu.VMEM((2 * rows, width), F32),
                pltpu.VMEM((2 * rows, width), BF16),
                pltpu.VMEM((2 * rows, width), BF16),
                pltpu.VMEM((tokens, width), BF16),
                pltpu.VMEM((3, 2, 64, 256), F32),
                pltpu.VMEM((3, 64, 256), F32),
                pltpu.VMEM((3, 64, 256), F32),
                pltpu.VMEM((3, 64, 256), F32),
                pltpu.VMEM((3, 2, 64, 256), BF16),
                pltpu.VMEM((2, 8, 128), F32),
                pltpu.VMEM((3, 2, 8, 128), F32),
                pltpu.VMEM((2, 2, 64, 128), F32),
                pltpu.VMEM((chunks, tokens, CW), BF16),
                pltpu.VMEM((2, 256, 128), BF16),
                pltpu.VMEM((chunks, 8, 64, CW), BF16),
                pltpu.VMEM((chunks, 7, 64, CW), BF16),
                pltpu.VMEM((chunks, 64, CW), BF16),
                pltpu.VMEM((chunks, 64, CW), BF16),
                pltpu.VMEM((chunks, 64, CW), F32),
                pltpu.VMEM((chunks, 8, CW), F32),
                pltpu.VMEM((chunks, 7, 8, CW), F32),
                pltpu.VMEM((chunks, 64, CW), BF16),
                dma((11,)),
                dma((3,)), dma((3,)), dma((3,)), dma((3,)), dma((3,)), dma((3,)), dma((3,)), dma((3,)),
                dma((chunks,)), dma((chunks,)), dma,
                dma((chunks,)), dma((chunks,)), dma((chunks,)), dma((chunks,)),
                dma((chunks,)), dma((chunks,)), dma((chunks,)),
            ],
            compiler_params=pltpu.CompilerParams(collective_id=0, has_side_effects=True),
            name="section_pair",
        )(
            enter_fwd.reshape(tokens, width),
            enter_rev.reshape(tokens, width),
            cot_rev.reshape(tokens, width),
            gain.reshape(2, width),
            proj_down.reshape(2, latent, width),
            proj_up.reshape(2, latent, width),
            master.reshape(2 * rows, width),
            moment.reshape(2 * rows, width),
            second.reshape(2 * rows, width),
        )
        return (
            leave.reshape(1, tokens, width),
            codes.reshape(2, 1, rows, width),
            scales.reshape(2, 1, 2, width // 128),
        )

    in_specs = (
        P("pipe", "expert", "dp"),
        P("pipe", "expert", "dp"),
        P("pipe", "expert", "dp"),
        P(None, "pipe", "dp"),
        P(None, "pipe", None, "dp"),
        P(None, "pipe", None, "dp"),
        P(None, "pipe", "expert", "dp"),
        P(None, "pipe", "expert", "dp"),
        P(None, "pipe", "expert", "dp"),
    )
    out_specs = (
        P("pipe", "expert", "dp"),
        P(None, "pipe", "expert", "dp"),
        P(None, "pipe", None, "dp"),
    )
    return jax.shard_map(shards, mesh=mesh, in_specs=in_specs, out_specs=out_specs, check_vma=False)
```

time: 395 us -> 106 us (0.27)
  waiting for transfers between devices: 277 us -> 0 us
  Pallas kernels: 0 us -> 99.8 us
  starting transfers between devices: 51.1 us -> 0 us
  blocking collectives: 33.8 us -> 0 us
  between operations: 14.2 us -> 0.64 us
  matrix products: 10.7 us -> 0 us
  other arithmetic: 4.79 us -> 0 us
    reduce_scatter x1 -> x0, waiting for transfers between devices: 113 us -> none  [shards(): lax.psum_scatter(jnp.concatenate([grad_down, grad_up], axis=1).astype(jnp...]
    pallas_call x0 -> x1, Pallas kernels: none -> 99.8 us  [shards(): pl.pallas_call(functools.partial(kernel, sections, chunks), out_shape=(ja...]
    ppermute x6 -> x0, waiting for transfers between devices: 90.2 us -> none  [the longest x5 90.2 us: from_partner(): return lax.ppermute(block, axis, route)]
    psum x1 -> x0, waiting for transfers between devices: 73.7 us -> none  [shards(): lax.psum((fwd_raw, fwd_squares, back_raw, back_squares, back_dlat), 'dp')]
    ppermute x6 -> x0, starting transfers between devices: 51 us -> none  [the longest x5 49.7 us: from_partner(): return lax.ppermute(block, axis, route)]
    all_gather x1 -> x0, blocking collectives: 27.6 us -> none  [shards(): gathered = lax.all_gather(local_peak[None], 'expert', axis=0, tiled=True)]
    dot_general x6 -> x0, matrix products: 10.7 us -> none  [the longest x2 4.8 us: prepare(): jnp.einsum('td,rd->tr', scaled, down, preferred_element_type=jnp.float32)]
    psum x1 -> x0, blocking collectives: 6.21 us -> none  [shards(): lax.psum((fwd_raw, fwd_squares, back_raw, back_squares, back_dlat), 'dp')]
  transfers between devices with their start and end apart: 8 -> 0, of which waited for: 7 -> 0; matrix products, arithmetic and copies ran while one was open for 1% -> 0% of each run, Pallas kernels for 0% -> 0%
where the time goes in v1:
time: 106 us; the launch traced here: 105 us
  Pallas kernels  99.8 us (94%)
  local copies, waits for them, and re-layouts  4.7 us (4%)
    pallas_call x1, Pallas kernels, shards(): pl.pallas_call(functools.partial(kernel, sections, chunks), out_shape=(ja...  99.8 us
    unnamed x3, local copies, waits for them, and re-layouts  4.7 us

profile of v1, /device:TPU:6, one launch (start us, length us, event | category | flops | bytes accessed | tf_op | source)
XLA Modules:
  0.0 105.1 jit_solution(3315090394553075782)
XLA Ops:
  0.6 99.8 %section_pair.1 = (bf16[128,1792]{1,0:T(8,128)(2,1)}, bf16[64,1792]{1,0:T(8,128)(2,1)}, f32[2,2,14]{2,1,0:T(2,128)}) custom-call(bf16[128,1792]{1,0:T(8,128)(2,1)} %bitcast.19, bf16[128,1792]{1,0:T(8,128)(2,1)} %bitcast.20, bf16[128,1792]{1,0:T(8,128)(2,1)} %bitcast.21, bf16[2,1792]{1,0:T(2,128)(2,1)} %bitcast.26, bf16[2,256,1792]{2,1,0:T(8,128)(2,1)} %bitcast.16, ...), custom_call_target="tpu_custom_call" | custom-call | tf_op jit(solution)/shard_map/section_pair/pallas_call | solution.py:279
  100.4 1.8 %copy.17 = bf16[1,128,1792]{2,1,0:T(8,128)(2,1)} copy(bf16[1,128,1792]{2,1,0:T(8,128)(2,1)} %bitcast.18) | data formatting | bytes 917504
  102.2 1.6 %copy.18 = bf16[2,1,32,1792]{3,2,1,0:T(8,128)(2,1)} copy(bf16[2,1,32,1792]{3,2,1,0:T(8,128)(2,1)} %bitcast.23) | data formatting | bytes 458752
  103.9 1.2 %copy.19 = f32[2,1,2,14]{3,2,1,0:T(2,128)} copy(f32[2,1,2,14]{3,2,1,0:T(2,128)} %bitcast.27) | data formatting | bytes 448

commit v2 on v1

--- a/solution.py
+++ b/solution.py
@@ -18,13 +18,13 @@
 def kernel(
     sections, chunks,
     x1_hbm, x2_hbm, c2_hbm, gain_hbm, down_hbm, up_hbm, master_hbm, moment_hbm, second_hbm,
-    leave_hbm, codes_hbm, scales_ref,
+    leave, coded, scales_ref,
     x1, x2, c2, gain, down, up, master, moment, second,
     xg2, part, core_got, chip_sum, near_got, lat, sq, sq_got, rows_r,
-    ybuf, turned, grads, group_got, share, mirror_got, fresh, peak, peak_got, coded,
+    ybuf, turned, grads, group_got, share, mirror_got, fresh, peak, peak_got,
     load_sem, core_send, core_recv, near_send, near_recv, lat_send, lat_recv, sq_send, sq_recv,
-    y_send, y_recv, zero_sem, group_send, group_recv, mirror_send, mirror_recv,
-    peak_send, peak_recv, code_sem,
+    y_send, y_recv, group_send, group_recv, mirror_send, mirror_recv,
+    peak_send, peak_recv,
 ):
     pipe = lax.axis_index("pipe")
     expert = lax.axis_index("expert")
@@ -45,9 +45,9 @@
                 peers.append(lax.rem(x_hi + dx, 2) * 4 + lax.rem(y + dy, 4))
 
     loads = [
-        (x1_hbm, x1), (gain_hbm, gain), (down_hbm.at[0], down.at[0]),
-        (x2_hbm, x2), (down_hbm.at[1], down.at[1]), (c2_hbm, c2), (up_hbm.at[1], up.at[1]),
-        (up_hbm.at[0], up.at[0]), (master_hbm, master), (moment_hbm, moment), (second_hbm, second),
+        (x2_hbm, x2), (gain_hbm, gain), (down_hbm.at[1], down.at[1]), (c2_hbm, c2), (up_hbm.at[1], up.at[1]),
+        (x1_hbm, x1), (down_hbm.at[0], down.at[0]), (up_hbm.at[0], up.at[0]),
+        (master_hbm, master), (moment_hbm, moment), (second_hbm, second),
     ]
     copies = [pltpu.make_async_copy(s, d, load_sem.at[i]) for i, (s, d) in enumerate(loads)]
     for copy in copies:
@@ -78,69 +78,64 @@
 
     for i in range(3):
         copies[i].wait()
-    _, raw, square = project(x1, gain[0:1, :].astype(F32), down[0])
-    part[0] = raw.reshape(2, 64, 256)
-    sq[0] = spread(square)
-    for i in range(3, 5):
-        copies[i].wait()
     scaled, raw, square = project(x2, gain[1:2, :].astype(F32), down[1])
     xg2[...] = scaled
     part[1] = raw.reshape(2, 64, 256)
     sq[1] = spread(square)
-    for i in range(5, 7):
+    for i in range(3, 5):
         copies[i].wait()
     raw = lax.dot_general(c2[...], up[1], NT, preferred_element_type=F32)
     part[2] = raw.reshape(2, 64, 256)
 
     pl.semaphore_wait(barrier, len(others))
 
-    pending = []
-    for i in range(3):
-        pending.append(send(part.at[i, 1 - core], core_got.at[i], core_send.at[i], core_recv.at[i], other_core))
-    for i, device in enumerate((other_core, near, near_other)):
-        pending.append(send(sq, sq_got.at[i], sq_send.at[i], sq_recv.at[i], device))
-    near_copies = []
-    for i in range(3):
-        pending[i].wait_recv()
+    core_copies, near_copies, lat_copies, sq_copies = {}, {}, {}, {}
+
+    def to_core(i):
+        core_copies[i] = send(part.at[i, 1 - core], core_got.at[i], core_send.at[i], core_recv.at[i], other_core)
+
+    def squares(s):
+        for i, device in enumerate((other_core, near, near_other)):
+            sq_copies[s, i] = send(sq.at[s], sq_got.at[i, s], sq_send.at[s, i], sq_recv.at[s, i], device)
+
+    def to_near(i):
+        core_copies[i].wait_recv()
         chip_sum[i] = part[i, core] + core_got[i]
-        near_copies.append(send(chip_sum.at[i], near_got.at[i], near_send.at[i], near_recv.at[i], near))
-    for i in range(3, 6):
-        pending[i].wait_recv()
-    for s in range(2):
+        near_copies[i] = send(chip_sum.at[i], near_got.at[i], near_send.at[i], near_recv.at[i], near)
+
+    def norms(s):
+        for i in range(3):
+            sq_copies[s, i].wait_recv()
         total = (sq[s] + sq_got[0, s]) + (sq_got[1, s] + sq_got[2, s])
         scale = lax.rsqrt(total / D + 1e-06)
-        turned_rows = jnp.broadcast_to(scale[0:1], (128, 128)).T
-        rows_r[s] = turned_rows.reshape(2, 64, 128)
-    lat_copies = []
-    for i in range(3):
+        rows_r[s] = jnp.broadcast_to(scale[0:1], (128, 128)).T.reshape(2, 64, 128)
+
+    def latents(i):
         near_copies[i].wait_recv()
         r = rows_r[min(i, 1), core]
         total = chip_sum[i] + near_got[i]
         lat[i, core] = (total * jnp.concatenate([r, r], axis=1)).astype(BF16)
-        lat_copies.append(send(lat.at[i, core], lat.at[i, core], lat_send.at[i], lat_recv.at[i], other_core))
-
-    copies[7].wait()
-    lat_copies[0].wait_recv()
-    hidden = lat[0].reshape(128, 256)
+        lat_copies[i] = send(lat.at[i, core], lat.at[i, core], lat_send.at[i], lat_recv.at[i], other_core)
+
+    to_core(1)
+    to_core(2)
+    squares(1)
+    for i in range(5, 7):
+        copies[i].wait()
+    _, raw, square = project(x1, gain[0:1, :].astype(F32), down[0])
+    part[0] = raw.reshape(2, 64, 256)
+    sq[0] = spread(square)
+    to_core(0)
+    squares(0)
+    to_near(1)
+    to_near(2)
+    to_near(0)
+    norms(1)
+    latents(1)
+    latents(2)
 
     def columns(k):
         return pl.ds(pl.multiple_of(k * CW, CW), CW)
-
-    def y_copy(k):
-        return pltpu.make_async_remote_copy(
-            src_ref=ybuf.at[k], dst_ref=leave_hbm.at[:, columns(k)],
-            send_sem=y_send.at[k], recv_sem=y_recv.at[k],
-            device_id=following, device_id_type=MESH,
-        )
-
-    @pl.loop(0, chunks)
-    def _(k):
-        wide = jnp.dot(hidden, up[0, :, columns(k)], preferred_element_type=F32)
-        ybuf[k] = (x1[:, columns(k)].astype(F32) + wide).astype(BF16)
-
-        @pl.when(pipe < sections - 1)
-        def _():
-            y_copy(k).start()
 
     for i in (1, 2):
         lat_copies[i].wait_recv()
@@ -154,6 +149,28 @@
         grads[k, :, 32:64, :] = grad_up.astype(BF16).reshape(8, 32, CW)
         for slot, peer in enumerate(peers):
             send(grads.at[k, peer], group_got.at[k, slot], group_send.at[k], group_recv.at[k], {"expert": peer})
+
+    copies[7].wait()
+    norms(0)
+    latents(0)
+    lat_copies[0].wait_recv()
+    hidden = lat[0].reshape(128, 256)
+
+    def y_copy(k):
+        return pltpu.make_async_remote_copy(
+            src_ref=ybuf.at[k], dst_ref=leave.at[k],
+            send_sem=y_send.at[k], recv_sem=y_recv.at[k],
+            device_id=following, device_id_type=MESH,
+        )
+
+    @pl.loop(0, chunks)
+    def _(k):
+        wide = jnp.dot(hidden, up[0, :, columns(k)], preferred_element_type=F32)
+        ybuf[k] = (x1[:, columns(k)].astype(F32) + wide).astype(BF16)
+
+        @pl.when(pipe < sections - 1)
+        def _():
+            y_copy(k).start()
 
     def mirror_copy(k):
         return pltpu.make_async_remote_copy(
@@ -192,9 +209,6 @@
             send(peak.at[k], peak_got.at[k, slot], peak_send.at[k], peak_recv.at[k], {"expert": peer})
 
     lane = lax.broadcasted_iota(jnp.int32, (8, 128), 1)
-
-    def code_copy(k):
-        return pltpu.make_async_copy(coded.at[k], codes_hbm.at[:, columns(k)], code_sem.at[k])
 
     def finish(k, tables):
         pltpu.make_async_copy(peak_got.at[k], peak_got.at[k], peak_recv.at[k]).wait()
@@ -214,38 +228,31 @@
             their_table = jnp.where(here, far, their_table)
             coded[k, 0:32, cols] = (fresh[k, 0:32, cols] / own[0:1]).astype(BF16)
             coded[k, 32:64, cols] = (fresh[k, 32:64, cols] / own[4:5]).astype(BF16)
-        code_copy(k).start()
         return mine_table, their_table
 
-    update(0)
+    @pl.loop(0, chunks)
+    def _(k):
+        update(k)
+
     empty = jnp.zeros((8, 128), F32)
-
-    def both(k, tables):
-        update(k)
-        return finish(k - 1, tables)
-
-    tables = lax.fori_loop(1, chunks, both, (empty, empty))
-    mine_table, their_table = finish(chunks - 1, tables)
+    mine_table, their_table = lax.fori_loop(0, chunks, finish, (empty, empty))
     width = scales_ref.shape[-1]
     for m in range(2):
         for rb in range(2):
             row = jnp.where(x_hi == rb, mine_table[4 * m : 4 * m + 1], their_table[4 * m : 4 * m + 1])
             scales_ref[m, rb : rb + 1, :] = row[:, 0:width]
 
-    for copy in pending + near_copies + lat_copies:
-        copy.wait_send()
+    for group in (core_copies, near_copies, lat_copies, sq_copies):
+        for copy in group.values():
+            copy.wait_send()
 
     @pl.when(pipe == 0)
     def _():
-        ybuf_zero = jnp.zeros((128, CW), BF16)
+        leave[...] = jnp.zeros_like(leave)
 
         @pl.loop(0, chunks)
         def _(k):
             y_copy(k).wait_send()
-            ybuf[k] = ybuf_zero
-            copy = pltpu.make_async_copy(ybuf.at[k], leave_hbm.at[:, columns(k)], zero_sem)
-            copy.start()
-            copy.wait()
 
     @pl.when(pipe > 0)
     def _():
@@ -262,7 +269,18 @@
         pltpu.make_async_copy(group_got.at[k], group_got.at[k], group_send.at[k]).wait()
         pltpu.make_async_copy(peak_got.at[k], peak_got.at[k], peak_send.at[k]).wait()
         mirror_copy(k).wait_send()
-        code_copy(k).wait()
+
+
+def store(chunks, leave, coded, scales, leave_hbm, codes_hbm, scales_hbm, sem):
+    copies = [pltpu.make_async_copy(scales, scales_hbm, sem.at[2 * chunks])]
+    for k in range(chunks):
+        cols = slice(k * CW, k * CW + CW)
+        copies.append(pltpu.make_async_copy(leave.at[k], leave_hbm.at[:, cols], sem.at[2 * k]))
+        copies.append(pltpu.make_async_copy(coded.at[k], codes_hbm.at[:, cols], sem.at[2 * k + 1]))
+    for copy in copies:
+        copy.start()
+    for copy in copies:
+        copy.wait()
 
 
 def solution(mesh):
@@ -275,16 +293,17 @@
         rows = master.shape[2]
         chunks = width // CW
         any_spec = pl.BlockSpec(memory_space=pl.ANY)
+        vmem_spec = pl.BlockSpec(memory_space=pltpu.VMEM)
         dma = pltpu.SemaphoreType.DMA
         leave, codes, scales = pl.pallas_call(
             functools.partial(kernel, sections, chunks),
             out_shape=(
-                jax.ShapeDtypeStruct((tokens, width), BF16),
-                jax.ShapeDtypeStruct((2 * rows, width), BF16),
-                jax.ShapeDtypeStruct((2, 2, width // 128), F32),
+                pltpu.VMEM((chunks, tokens, CW), BF16),
+                pltpu.VMEM((chunks, 2 * rows, CW), BF16),
+                pltpu.VMEM((2, 2, width // 128), F32),
             ),
             in_specs=[any_spec] * 9,
-            out_specs=(any_spec, any_spec, pl.BlockSpec(memory_space=pltpu.VMEM)),
+            out_specs=(vmem_spec,) * 3,
             scratch_shapes=[
                 pltpu.VMEM((tokens, width), BF16),
                 pltpu.VMEM((tokens, width), BF16),
@@ -313,12 +332,11 @@
                 pltpu.VMEM((chunks, 64, CW), F32),
                 pltpu.VMEM((chunks, 8, CW), F32),
                 pltpu.VMEM((chunks, 7, 8, CW), F32),
-                pltpu.VMEM((chunks, 64, CW), BF16),
                 dma((11,)),
-                dma((3,)), dma((3,)), dma((3,)), dma((3,)), dma((3,)), dma((3,)), dma((3,)), dma((3,)),
-                dma((chunks,)), dma((chunks,)), dma,
+                dma((3,)), dma((3,)), dma((3,)), dma((3,)), dma((3,)), dma((3,)), dma((2, 3)), dma((2, 3)),
+                dma((chunks,)), dma((chunks,)),
                 dma((chunks,)), dma((chunks,)), dma((chunks,)), dma((chunks,)),
-                dma((chunks,)), dma((chunks,)), dma((chunks,)),
+                dma((chunks,)), dma((chunks,)),
             ],
             compiler_params=pltpu.CompilerParams(collective_id=0, has_side_effects=True),
             name="section_pair",
@@ -333,6 +351,19 @@
             moment.reshape(2 * rows, width),
             second.reshape(2 * rows, width),
         )
+        leave, codes, scales = pl.pallas_call(
+            functools.partial(store, chunks),
+            out_shape=(
+                jax.ShapeDtypeStruct((tokens, width), BF16),
+                jax.ShapeDtypeStruct((2 * rows, width), BF16),
+                jax.ShapeDtypeStruct((2, 2, width // 128), F32),
+            ),
+            in_specs=[vmem_spec] * 3,
+            out_specs=(any_spec,) * 3,
+            scratch_shapes=[dma((2 * chunks + 1,))],
+            compiler_params=pltpu.CompilerParams(vmem_limit_bytes=1 << 20),
+            name="store_outputs",
+        )(leave, codes, scales)
         return (
             leave.reshape(1, tokens, width),
             codes.reshape(2, 1, rows, width),

time: 106 us -> 89.3 us (0.84)
  Pallas kernels: 99.8 us -> 87.3 us
  local copies, waits for them, and re-layouts: 4.7 us -> 0 us
    pallas_call x1 -> x2, Pallas kernels: 99.8 us -> 87.3 us  [the longest x1 86.3 us: shards(): pl.pallas_call(functools.partial(kernel, sections, chunks), out_shape=(pl...]
    unnamed x3 -> x0, local copies, waits for them, and re-layouts: 4.7 us -> none
where the time goes in v2:
time: 89.3 us; the launch traced here: 87.9 us
  Pallas kernels  87.3 us (98%)
    pallas_call x1, Pallas kernels, shards(): pl.pallas_call(functools.partial(kernel, sections, chunks), out_shape=(pl...  86.3 us

profile of v2, /device:TPU:6, one launch (start us, length us, event | category | flops | bytes accessed | tf_op | source)
XLA Modules:
  0.0 87.9 jit_solution(17543175458789657048)
XLA Ops:
  0.6 86.3 %section_pair.1 = (bf16[7,128,256]{2,1,0:T(8,128)(2,1)S(1)}, bf16[7,64,256]{2,1,0:T(8,128)(2,1)S(1)}, f32[2,2,14]{2,1,0:T(2,128)S(1)}) custom-call(bf16[128,1792]{1,0:T(8,128)(2,1)} %bitcast.18, bf16[128,1792]{1,0:T(8,128)(2,1)} %bitcast.19, bf16[128,1792]{1,0:T(8,128)(2,1)} %bitcast.20, bf16[2,1792]{1,0:T(2,128)(2,1)} %bitcast.24, ...), custom_call_target="tpu_custom_call" | custom-call | tf_op jit(solution)/shard_map/section_pair/pallas_call | solution.py:298
  87.0 1.0 %store_outputs.1 = (bf16[128,1792]{1,0:T(8,128)(2,1)}, bf16[64,1792]{1,0:T(8,128)(2,1)}, f32[2,2,14]{2,1,0:T(2,128)}) custom-call(bf16[7,128,256]{2,1,0:T(8,128)(2,1)S(1)} %get-tuple-element.9.leave, bf16[7,64,256]{2,1,0:T(8,128)(2,1)S(1)} %get-tuple-element.10.coded, f32[2,2,14]{2,1,0:T(2,128)S(1)} %get-tuple-element.11.scales), custom_call_target="tpu_custom_call" | custom-call | tf_op jit(solution)/shard_map/store_outputs/pallas_call | solution.py:354
